TPU v7x, 512 devices: a whole 4x4x16 slice. The times are simulated.
512 devices in a mesh: gx: 32 (over y, x, z_hi), gy: 8 (over z_lo), gz: 2 (over core).
Axes of the slice: x: 4, y: 4, z: 16 (z_hi: 2, z_lo: 8; z = z_hi * 8 + z_lo), core: 2. Of those that a mesh axis runs over, the one named last changes fastest.
Arguments:
- source: float32 [256, 64, 4096], P('gx', 'gz', 'gy'), may hold values from -24 to 24
- coef: float32 [256, 64, 128], P('gx', 'gz', 'gy'), may hold values from 0.01 to 0.05
- face_trace: int32 [256, 2, 128], P('gx', 'gz'), may hold values from 0 to 1023, as said below
- near_col: int32 [32, 2, 8], P('gx', 'gz', 'gy'), may hold values from 0 to 63, as said below
- far_col: int32 [32, 2, 8, 7], P('gx', 'gz', 'gy'), may hold values from 0 to 63, as said below
- near_tile: bfloat16 [32, 2, 8, 1024, 1024], P('gx', 'gz', 'gy'), may hold values from -0.1875 to 0.1875
- far_u: bfloat16 [32, 2, 8, 7, 16, 1024], P('gx', 'gz', 'gy'), may hold values from -0.1875 to 0.1875
- far_v: bfloat16 [32, 2, 8, 7, 16, 1024], P('gx', 'gz', 'gy'), may hold values from -0.1875 to 0.1875
Outputs:
- solution: float32 [256, 64, 4096], P('gx', 'gz', 'gy')
- flux: float32 [256, 2, 4096], P('gx', 'gz', 'gy')
Inputs may be any that keep to these rules, and one draw needn't show every extreme that they name: For every block of 8 rows of x and each face s, the entries face_trace(x, s, y) of that block are a permutation of 0 to 1023. For every row block, near_col over the slots j together with far_col over j and k name each column block 0 to 63 exactly once. `far_col`: see near_col: near and far column blocks of a row block together name every column block exactly once.
All inputs are finite; a program needn't handle non-finite values.
Results may differ from a plain program's by a relative error of at most 0.003.
Values may be sent and summed in bfloat16 or wider, within the bound.
A program may use at most 64 MiB of HBM per device.

v0:
```python
import jax
import jax.numpy as jnp
from jax import lax
from jax.sharding import PartitionSpec as P

E = 32
SWEEPS = 3


def extended(block, sides, width):
    for axis, dim in sides:
        count = lax.axis_size(axis)
        forward = [(i, i + 1) for i in range(count - 1)]
        backward = [(target, source) for source, target in forward]
        low = lax.ppermute(
            lax.slice_in_dim(block, block.shape[dim] - width, None, axis=dim), axis, forward
        )
        high = lax.ppermute(lax.slice_in_dim(block, 0, width, axis=dim), axis, backward)
        block = jnp.concatenate([low, block, high], axis=dim)
    return block


def sweep(field, rhs, diag):
    slab = extended(field, (("gx", 0), ("gz", 1)), 1)
    pencil = extended(field, (("gy", 2),), E)
    beside = slab[2:, 1:-1] + slab[:-2, 1:-1] + slab[1:-1, 2:] + slab[1:-1, :-2]
    beside = beside + pencil[:, :, 2 * E :] + pencil[:, :, : -2 * E]
    return (rhs + beside) / diag


def body(source, coef, face_trace, near_col, far_col, near_tile, far_u, far_v):
    rows_x = source.shape[0]
    depth = source.shape[1]
    cells_y = coef.shape[2]
    groups = lax.axis_size("gy")
    mine_y = lax.axis_index("gy")
    face_side = lax.axis_index("gz")
    tile = near_tile.shape[3]
    far_count = far_u.shape[3]
    rank = far_u.shape[4]
    diag = jnp.repeat(6.0 + coef, E, axis=2)
    field = jnp.zeros(source.shape, jnp.float32)
    for step in range(SWEEPS):
        field = sweep(field, source, diag)
    plane = jnp.where(face_side == 0, 0, depth - 1)
    depth_ids = jnp.arange(depth, dtype=jnp.int32)
    plane_mask = (depth_ids == plane).astype(jnp.float32)
    face_local = jnp.where(face_side == 0, field[:, 0, :], field[:, depth - 1, :]).astype(
        jnp.bfloat16
    )
    face_block = lax.all_gather(face_local, "gy", axis=1, tiled=True)
    perm = face_trace.reshape(tile)
    inverse = jnp.zeros((tile,), jnp.int32).at[perm].set(jnp.arange(tile, dtype=jnp.int32))
    block_traces = face_block.reshape(tile, E)[inverse].T
    wanted = jnp.concatenate([near_col.reshape(1), far_col.reshape(far_count)])
    piece = lax.all_gather(block_traces[None], ("gx", "gz"), axis=0, tiled=True)
    numbers = jnp.arange(piece.shape[0], dtype=jnp.int32)
    onehot = (wanted[:, None] == numbers[None, :]).astype(jnp.bfloat16)
    chosen = jnp.einsum("cn,net->cet", onehot, piece, preferred_element_type=jnp.float32).astype(
        jnp.bfloat16
    )
    nearpart = lax.dot_general(
        chosen[0],
        near_tile.reshape(tile, tile),
        (((1,), (1,)), ((), ())),
        preferred_element_type=jnp.float32,
    )
    weights = jnp.einsum(
        "fet,frt->fer",
        chosen[1:],
        far_v.reshape(far_count, rank, tile),
        preferred_element_type=jnp.float32,
    ).astype(jnp.bfloat16)
    farpart = jnp.einsum(
        "fer,frt->et",
        weights,
        far_u.reshape(far_count, rank, tile),
        preferred_element_type=jnp.float32,
    )
    partial_rows = nearpart + farpart
    total = lax.psum(partial_rows, "gy")
    face_flux = total[:, perm].reshape(E, rows_x, cells_y * groups)
    mine = lax.dynamic_slice_in_dim(face_flux, mine_y * cells_y, cells_y, 2)
    flux_rows = mine.transpose(1, 2, 0).reshape(rows_x, cells_y * E)
    extra = plane_mask[None, :, None] * flux_rows[:, None, :]
    solution = sweep(field, source + extra, diag)
    return (solution, flux_rows[:, None, :])


def solution(mesh):
    return jax.shard_map(
        body,
        mesh=mesh,
        in_specs=(
            P("gx", "gz", "gy"),
            P("gx", "gz", "gy"),
            P("gx", "gz", None),
            P("gx", "gz", "gy"),
            P("gx", "gz", "gy", None),
            P("gx", "gz", "gy", None, None),
            P("gx", "gz", "gy", None, None, None),
            P("gx", "gz", "gy", None, None, None),
        ),
        out_specs=(P("gx", "gz", "gy"), P("gx", "gz", "gy")),
        check_vma=False,
    )
```

profile of v0, /device:TPU:2, one launch (start us, length us, event | category | flops | bytes accessed | tf_op | source)
XLA Modules:
  0.0 448.9 jit_solution(9452833639911425397)
XLA Ops:
  7.2 15.8 %collective-permute-start = (f32[1,32,512]{2,1,0:T(8,128)S(1)}, f32[1,32,512]{2,1,0:T(8,128)S(1)}, u32[]{:S(2)}, u32[]{:S(2)}) collective-permute-start(f32[1,32,512]{2,1,0:T(8,128)S(1)} %broadcast.45), channel_id=1, source_target_pairs={{16,0},{32,16},{48,32},{64,48},{80,64},{96,80},{112,96},{128,112},... | collective-permute-start | bytes 196616 | tf_op jit(solution)/shard_map/ppermute | solution.py:18
  23.1 1.9 collective-permute-start.1
  27.0 5.2 %collective-permute-start.5 = (f32[8,32,32]{2,1,0:T(8,128)}, f32[8,32,32]{2,1,0:T(8,128)}, u32[]{:S(2)}, u32[]{:S(2)}) collective-permute-start(f32[8,32,32]{2,1,0:T(8,128)} %broadcast.46), channel_id=1, source_target_pairs={{0,2},{2,4},{4,6},{6,8},{8,10},{10,12},{12,14},{1,3},{3,5},{5,7},{... | collective-permute-start | bytes 98312 | tf_op jit(solution)/shard_map/ppermute | solution.py:15
  32.2 7.6 %collective-permute-done.1 = f32[1,32,512]{2,1,0:T(8,128)S(1)} collective-permute-done((f32[1,32,512]{2,1,0:T(8,128)S(1)}, f32[1,32,512]{2,1,0:T(8,128)S(1)}, u32[]{:S(2)}, u32[]{:S(2)}) %collective-permute-start.1) | collective-permute-done | bytes 65568 | tf_op jit(solution)/shard_map/ppermute | solution.py:15
  41.2 3.0 collective-permute-start.3
  45.2 2.0 broadcast_in_dim.18
  47.2 2.3 reshape.71
  51.2 5.9 %collective-permute-start.6 = (f32[1,32,512]{2,1,0:T(8,128)S(1)}, f32[1,32,512]{2,1,0:T(8,128)S(1)}, u32[]{:S(2)}, u32[]{:S(2)}) collective-permute-start(f32[1,32,512]{2,1,0:T(8,128)S(1)} %get-tuple-element.19), channel_id=1, source_target_pairs={{16,0},{32,16},{48,32},{64,48},{80,64},{96,80},{112,96},{128,112},... | collective-permute-start | bytes 196616 | tf_op jit(solution)/shard_map/ppermute | solution.py:18
  57.1 8.6 %collective-permute-start.7 = (f32[1,32,512]{2,1,0:T(8,128)S(1)}, f32[1,32,512]{2,1,0:T(8,128)S(1)}, u32[]{:S(2)}, u32[]{:S(2)}) collective-permute-start(f32[1,32,512]{2,1,0:T(8,128)S(1)} %get-tuple-element.18), channel_id=1, source_target_pairs={{0,16},{16,32},{32,48},{48,64},{64,80},{80,96},{96,112},{112,128},... | collective-permute-start | bytes 196616 | tf_op jit(solution)/shard_map/ppermute | solution.py:15
  67.8 6.8 %collective-permute-start.11 = (f32[8,32,32]{2,1,0:T(8,128)}, f32[8,32,32]{2,1,0:T(8,128)S(1)}, u32[]{:S(2)}, u32[]{:S(2)}) collective-permute-start(f32[8,32,32]{2,1,0:T(8,128)} %get-tuple-element.21), channel_id=1, source_target_pairs={{0,2},{2,4},{4,6},{6,8},{8,10},{10,12},{12,14},{1,3},{3,5},{5,7},{... | collective-permute-start | bytes 98312 | tf_op jit(solution)/shard_map/ppermute | solution.py:15
  76.5 4.2 collective-permute-start.9
  81.4 4.3 scatter_custom_fusion
  85.8 2.9 fusion.31
  88.7 4.6 %collective-permute-start.12 = (f32[1,32,512]{2,1,0:T(8,128)S(1)}, f32[1,32,512]{2,1,0:T(8,128)S(1)}, u32[]{:S(2)}, u32[]{:S(2)}) collective-permute-start(f32[1,32,512]{2,1,0:T(8,128)S(1)} %get-tuple-element.15), channel_id=1, source_target_pairs={{16,0},{32,16},{48,32},{64,48},{80,64},{96,80},{112,96},{128,112},... | collective-permute-start | bytes 196616 | tf_op jit(solution)/shard_map/ppermute | solution.py:18
  93.3 9.9 %collective-permute-start.13 = (f32[1,32,512]{2,1,0:T(8,128)S(1)}, f32[1,32,512]{2,1,0:T(8,128)S(1)}, u32[]{:S(2)}, u32[]{:S(2)}) collective-permute-start(f32[1,32,512]{2,1,0:T(8,128)S(1)} %get-tuple-element.14), channel_id=1, source_target_pairs={{0,16},{16,32},{32,48},{48,64},{64,80},{80,96},{96,112},{112,128},... | collective-permute-start | bytes 196616 | tf_op jit(solution)/shard_map/ppermute | solution.py:15
  105.3 6.3 %collective-permute-start.17 = (f32[8,32,32]{2,1,0:T(8,128)}, f32[8,32,32]{2,1,0:T(8,128)S(1)}, u32[]{:S(2)}, u32[]{:S(2)}) collective-permute-start(f32[8,32,32]{2,1,0:T(8,128)} %get-tuple-element.17), channel_id=1, source_target_pairs={{0,2},{2,4},{4,6},{6,8},{8,10},{10,12},{12,14},{1,3},{3,5},{5,7},{... | collective-permute-start | bytes 98312 | tf_op jit(solution)/shard_map/ppermute | solution.py:15
  113.6 4.2 collective-permute-start.15
  118.4 2.9 fusion.24
  122.1 42.9 %all-gather = bf16[8,1,4096]{2,1,0:T(2,128)(2,1)S(1)} all-gather(bf16[8,1,512]{2,1,0:T(2,128)(2,1)S(1)} %fusion.43), channel_id=2, replica_groups=mesh['gx'=32,'gy'=8,'gz'=2] {'gy'}, dimensions={2}, use_global_device_ids=true | all-gather | bytes 73728 | tf_op jit(solution)/shard_map/all_gather | solution.py:51
  165.5 4.3 gather_fusion
  173.9 3.7 collective-permute-start.18
  177.6 11.0 %collective-permute-start.19 = (f32[1,32,512]{2,1,0:T(8,128)}, f32[1,32,512]{2,1,0:T(8,128)S(1)}, u32[]{:S(2)}, u32[]{:S(2)}) collective-permute-start(f32[1,32,512]{2,1,0:T(8,128)} %get-tuple-element.10), channel_id=1, source_target_pairs={{0,16},{16,32},{32,48},{48,64},{64,80},{80,96},{96,112},{112,128},... | collective-permute-start | bytes 196616 | tf_op jit(solution)/shard_map/ppermute | solution.py:15
  188.6 117.6 %all-gather.4.cloned.1.call-done = bf16[2048,1024]{1,0:T(8,128)(2,1)} async-done(((bf16[32,1024]{1,0:T(8,128)(2,1)}), bf16[2048,1024]{1,0:T(8,128)(2,1)}) %all-gather.4.cloned.1.call-update) | async-done | bytes 4194320 | tf_op jit(solution)/shard_map/all_gather | solution.py:56
  306.2 6.7 %fusion.4 = bf16[8,32,1024]{2,0,1:T(8,128)(2,1)S(1)} fusion(bf16[64,32,1024]{2,1,0:T(8,128)(2,1)} %bitcast.35, s32[8]{0:T(128)S(1)} %pad_add_fusion), kind=kOutput, calls=%fused_computation.7 | convolution fusion | flops 33817088 | bytes 4718624 | tf_op jit(solution)/shard_map/cn,net->cet/dot_general | solution.py:59
  314.6 2.5 fusion.7
  317.2 1.7 fusion.51
  320.2 5.2 %collective-permute-start.23 = (f32[8,32,32]{2,1,0:T(8,128)}, f32[8,32,32]{2,1,0:T(8,128)}, u32[]{:S(2)}, u32[]{:S(2)}) collective-permute-start(f32[8,32,32]{2,1,0:T(8,128)} %get-tuple-element.13), channel_id=1, source_target_pairs={{0,2},{2,4},{4,6},{6,8},{8,10},{10,12},{12,14},{1,3},{3,5},{5,7},{... | collective-permute-start | bytes 98312 | tf_op jit(solution)/shard_map/ppermute | solution.py:15
  328.3 3.0 collective-permute-start.21
  331.3 98.3 %all-reduce.6.cloned.1.call-done = f32[32,1024]{1,0:T(8,128)} async-done(((f32[32,1024]{1,0:T(8,128)}), f32[32,1024]{1,0:T(8,128)}) %all-reduce.6.cloned.1.call-update) | async-done | bytes 131088 | tf_op jit(solution)/shard_map/psum | solution.py:81
  429.7 1.9 copy.20
  431.6 5.0 %gather_fusion.1 = f32[1024,32]{1,0:T(8,128)} fusion(f32[32,1024]{0,1:T(8,128)} %copy.20, s32[1024]{0:T(1024)S(1)} %broadcast_clamp_fusion), kind=kCustom, calls=%fused_computation.1 | custom fusion | bytes 266240 | tf_op jit(solution)/shard_map/gather | solution.py:82
  438.3 3.8 fusion.17
  (80 shorter events, 27.5 us)
Async XLA Ops:
  7.2 306.7 %copy-start = (bf16[1,1,1,1024,1024]{4,3,2,1,0:T(8,128)(2,1)S(1)}, bf16[1,1,1,1024,1024]{4,3,2,1,0:T(8,128)(2,1)}, u32[]{:S(2)}) copy-start(bf16[1,1,1,1024,1024]{4,3,2,1,0:T(8,128)(2,1)} %param.13) | copy-start | bytes 6291460
  7.2 42.3 %copy-start.1 = (f32[8,32,512]{2,1,0:T(8,128)S(1)}, f32[8,32,512]{2,1,0:T(8,128)}, u32[]{:S(2)}) copy-start(f32[8,32,512]{2,1,0:T(8,128)} %param.8) | copy-start | bytes 1572868
  7.2 299.1 %all-gather.4.cloned.1.call-start = ((), (), s32[]{:S(2)}) async-start(), calls=%async_computation.1 | async-start | bytes 4259840 | tf_op jit(solution)/shard_map/all_gather | solution.py:56
  7.2 25.0 %collective-permute-start = (f32[1,32,512]{2,1,0:T(8,128)S(1)}, f32[1,32,512]{2,1,0:T(8,128)S(1)}, u32[]{:S(2)}, u32[]{:S(2)}) collective-permute-start(f32[1,32,512]{2,1,0:T(8,128)S(1)} %broadcast.45), channel_id=1, source_target_pairs={{16,0},{32,16},{48,32},{64,48},{80,64},{96,80},{112,96},{128,112},... | collective-permute-start | bytes 196616 | tf_op jit(solution)/shard_map/ppermute | solution.py:18
  23.1 16.7 %collective-permute-start.1 = (f32[1,32,512]{2,1,0:T(8,128)S(1)}, f32[1,32,512]{2,1,0:T(8,128)S(1)}, u32[]{:S(2)}, u32[]{:S(2)}) collective-permute-start(f32[1,32,512]{2,1,0:T(8,128)S(1)} %broadcast.45), channel_id=1, source_target_pairs={{0,16},{16,32},{32,48},{48,64},{64,80},{80,96},{96,112},{112,128},... | collective-permute-start | bytes 196616 | tf_op jit(solution)/shard_map/ppermute | solution.py:15
  25.7 23.8 %collective-permute-start.4 = (f32[8,32,32]{2,1,0:T(8,128)}, f32[8,32,32]{2,1,0:T(8,128)}, u32[]{:S(2)}, u32[]{:S(2)}) collective-permute-start(f32[8,32,32]{2,1,0:T(8,128)} %broadcast.46), channel_id=1, source_target_pairs={{2,0},{4,2},{6,4},{8,6},{10,8},{12,10},{14,12},{3,1},{5,3},{7,5},{... | collective-permute-start | bytes 98312 | tf_op jit(solution)/shard_map/ppermute | solution.py:18
  27.0 22.5 %collective-permute-start.5 = (f32[8,32,32]{2,1,0:T(8,128)}, f32[8,32,32]{2,1,0:T(8,128)}, u32[]{:S(2)}, u32[]{:S(2)}) collective-permute-start(f32[8,32,32]{2,1,0:T(8,128)} %broadcast.46), channel_id=1, source_target_pairs={{0,2},{2,4},{4,6},{6,8},{8,10},{10,12},{12,14},{1,3},{3,5},{5,7},{... | collective-permute-start | bytes 98312 | tf_op jit(solution)/shard_map/ppermute | solution.py:15
  39.9 5.3 %copy-start.5 = (f32[8,32,512]{2,1,0:T(8,128)}, f32[8,32,512]{2,1,0:T(8,128)S(1)}, u32[]{:S(2)}) copy-start(f32[8,32,512]{2,1,0:T(8,128)S(1)} %broadcast_in_dim.8) | copy-start | bytes 1572868
  39.9 9.6 %collective-permute-start.2 = (f32[10,1,512]{2,1,0:T(1,128)S(1)}, f32[10,1,512]{2,1,0:T(1,128)S(1)}, u32[]{:S(2)}, u32[]{:S(2)}) collective-permute-start(f32[10,1,512]{2,1,0:T(1,128)S(1)} %get-tuple-element.8), channel_id=1, source_target_pairs={{1,0},{3,2},{5,4},{7,6},{9,8},{11,10},{13,12},{15,14},{17,16},{19,... | collective-permute-start | bytes 61448 | tf_op jit(solution)/shard_map/ppermute | solution.py:18
  41.2 8.3 %collective-permute-start.3 = (f32[10,1,512]{2,1,0:T(1,128)S(1)}, f32[10,1,512]{2,1,0:T(1,128)S(1)}, u32[]{:S(2)}, u32[]{:S(2)}) collective-permute-start(f32[10,1,512]{2,1,0:T(1,128)S(1)} %get-tuple-element.9), channel_id=1, source_target_pairs={{0,1},{2,3},{4,5},{6,7},{8,9},{10,11},{12,13},{14,15},{16,17},{18,... | collective-permute-start | bytes 61448 | tf_op jit(solution)/shard_map/ppermute | solution.py:15
  51.2 23.4 %copy-start.4 = (f32[8,32,512]{2,1,0:T(8,128)}, f32[8,32,512]{2,1,0:T(8,128)S(1)}, u32[]{:S(2)}) copy-start(f32[8,32,512]{2,1,0:T(8,128)S(1)} %fusion.14) | copy-start | bytes 1572868
  51.2 23.4 %collective-permute-start.6 = (f32[1,32,512]{2,1,0:T(8,128)S(1)}, f32[1,32,512]{2,1,0:T(8,128)S(1)}, u32[]{:S(2)}, u32[]{:S(2)}) collective-permute-start(f32[1,32,512]{2,1,0:T(8,128)S(1)} %get-tuple-element.19), channel_id=1, source_target_pairs={{16,0},{32,16},{48,32},{64,48},{80,64},{96,80},{112,96},{128,112},... | collective-permute-start | bytes 196616 | tf_op jit(solution)/shard_map/ppermute | solution.py:18
  57.1 17.5 %collective-permute-start.7 = (f32[1,32,512]{2,1,0:T(8,128)S(1)}, f32[1,32,512]{2,1,0:T(8,128)S(1)}, u32[]{:S(2)}, u32[]{:S(2)}) collective-permute-start(f32[1,32,512]{2,1,0:T(8,128)S(1)} %get-tuple-element.18), channel_id=1, source_target_pairs={{0,16},{16,32},{32,48},{48,64},{64,80},{80,96},{96,112},{112,128},... | collective-permute-start | bytes 196616 | tf_op jit(solution)/shard_map/ppermute | solution.py:15
  66.5 19.2 %collective-permute-start.10 = (f32[8,32,32]{2,1,0:T(8,128)}, f32[8,32,32]{2,1,0:T(8,128)S(1)}, u32[]{:S(2)}, u32[]{:S(2)}) collective-permute-start(f32[8,32,32]{2,1,0:T(8,128)} %get-tuple-element.20), channel_id=1, source_target_pairs={{2,0},{4,2},{6,4},{8,6},{10,8},{12,10},{14,12},{3,1},{5,3},{7,5},{... | collective-permute-start | bytes 98312 | tf_op jit(solution)/shard_map/ppermute | solution.py:18
  67.8 18.0 %collective-permute-start.11 = (f32[8,32,32]{2,1,0:T(8,128)}, f32[8,32,32]{2,1,0:T(8,128)S(1)}, u32[]{:S(2)}, u32[]{:S(2)}) collective-permute-start(f32[8,32,32]{2,1,0:T(8,128)} %get-tuple-element.21), channel_id=1, source_target_pairs={{0,2},{2,4},{4,6},{6,8},{8,10},{10,12},{12,14},{1,3},{3,5},{5,7},{... | collective-permute-start | bytes 98312 | tf_op jit(solution)/shard_map/ppermute | solution.py:15
  75.2 10.5 %collective-permute-start.8 = (f32[10,1,512]{2,1,0:T(1,128)}, f32[10,1,512]{2,1,0:T(1,128)}, u32[]{:S(2)}, u32[]{:S(2)}) collective-permute-start(f32[10,1,512]{2,1,0:T(1,128)} %get-tuple-element.6), channel_id=1, source_target_pairs={{1,0},{3,2},{5,4},{7,6},{9,8},{11,10},{13,12},{15,14},{17,16},{19,... | collective-permute-start | bytes 61448 | tf_op jit(solution)/shard_map/ppermute | solution.py:18
  76.5 9.3 %collective-permute-start.9 = (f32[10,1,512]{2,1,0:T(1,128)}, f32[10,1,512]{2,1,0:T(1,128)}, u32[]{:S(2)}, u32[]{:S(2)}) collective-permute-start(f32[10,1,512]{2,1,0:T(1,128)} %get-tuple-element.7), channel_id=1, source_target_pairs={{0,1},{2,3},{4,5},{6,7},{8,9},{10,11},{12,13},{14,15},{16,17},{18,... | collective-permute-start | bytes 61448 | tf_op jit(solution)/shard_map/ppermute | solution.py:15
  88.7 23.0 %copy-start.3 = (f32[8,32,512]{2,1,0:T(8,128)}, f32[8,32,512]{2,1,0:T(8,128)S(1)}, u32[]{:S(2)}) copy-start(f32[8,32,512]{2,1,0:T(8,128)S(1)} %fusion.31) | copy-start | bytes 1572868
  88.7 83.6 %copy-start.6 = (s32[1,1,1,7]{3,2,1,0:T(1,128)S(1)}, s32[1,1,1,7]{3,2,1,0:T(1,128)}, u32[]{:S(2)}) copy-start(s32[1,1,1,7]{3,2,1,0:T(1,128)} %param.12) | copy-start | bytes 88
  88.7 22.9 %collective-permute-start.12 = (f32[1,32,512]{2,1,0:T(8,128)S(1)}, f32[1,32,512]{2,1,0:T(8,128)S(1)}, u32[]{:S(2)}, u32[]{:S(2)}) collective-permute-start(f32[1,32,512]{2,1,0:T(8,128)S(1)} %get-tuple-element.15), channel_id=1, source_target_pairs={{16,0},{32,16},{48,32},{64,48},{80,64},{96,80},{112,96},{128,112},... | collective-permute-start | bytes 196616 | tf_op jit(solution)/shard_map/ppermute | solution.py:18
  93.3 18.3 %collective-permute-start.13 = (f32[1,32,512]{2,1,0:T(8,128)S(1)}, f32[1,32,512]{2,1,0:T(8,128)S(1)}, u32[]{:S(2)}, u32[]{:S(2)}) collective-permute-start(f32[1,32,512]{2,1,0:T(8,128)S(1)} %get-tuple-element.14), channel_id=1, source_target_pairs={{0,16},{16,32},{32,48},{48,64},{64,80},{80,96},{96,112},{112,128},... | collective-permute-start | bytes 196616 | tf_op jit(solution)/shard_map/ppermute | solution.py:15
  104.0 13.8 %collective-permute-start.16 = (f32[8,32,32]{2,1,0:T(8,128)}, f32[8,32,32]{2,1,0:T(8,128)S(1)}, u32[]{:S(2)}, u32[]{:S(2)}) collective-permute-start(f32[8,32,32]{2,1,0:T(8,128)} %get-tuple-element.16), channel_id=1, source_target_pairs={{2,0},{4,2},{6,4},{8,6},{10,8},{12,10},{14,12},{3,1},{5,3},{7,5},{... | collective-permute-start | bytes 98312 | tf_op jit(solution)/shard_map/ppermute | solution.py:18
  105.3 12.5 %collective-permute-start.17 = (f32[8,32,32]{2,1,0:T(8,128)}, f32[8,32,32]{2,1,0:T(8,128)S(1)}, u32[]{:S(2)}, u32[]{:S(2)}) collective-permute-start(f32[8,32,32]{2,1,0:T(8,128)} %get-tuple-element.17), channel_id=1, source_target_pairs={{0,2},{2,4},{4,6},{6,8},{8,10},{10,12},{12,14},{1,3},{3,5},{5,7},{... | collective-permute-start | bytes 98312 | tf_op jit(solution)/shard_map/ppermute | solution.py:15
  112.3 5.5 %collective-permute-start.14 = (f32[10,1,512]{2,1,0:T(1,128)}, f32[10,1,512]{2,1,0:T(1,128)}, u32[]{:S(2)}, u32[]{:S(2)}) collective-permute-start(f32[10,1,512]{2,1,0:T(1,128)} %get-tuple-element.4), channel_id=1, source_target_pairs={{1,0},{3,2},{5,4},{7,6},{9,8},{11,10},{13,12},{15,14},{17,16},{19,... | collective-permute-start | bytes 61448 | tf_op jit(solution)/shard_map/ppermute | solution.py:18
  113.6 4.8 %collective-permute-start.15 = (f32[10,1,512]{2,1,0:T(1,128)}, f32[10,1,512]{2,1,0:T(1,128)}, u32[]{:S(2)}, u32[]{:S(2)}) collective-permute-start(f32[10,1,512]{2,1,0:T(1,128)} %get-tuple-element.5), channel_id=1, source_target_pairs={{0,1},{2,3},{4,5},{6,7},{8,9},{10,11},{12,13},{14,15},{16,17},{18,... | collective-permute-start | bytes 61448 | tf_op jit(solution)/shard_map/ppermute | solution.py:15
  171.6 258.1 %all-reduce.6.cloned.1.call-start = ((), (), s32[]{:S(2)}) async-start(), calls=%async_computation | async-start | bytes 262144 | tf_op jit(solution)/shard_map/psum | solution.py:81
  173.9 151.5 %collective-permute-start.18 = (f32[1,32,512]{2,1,0:T(8,128)}, f32[1,32,512]{2,1,0:T(8,128)S(1)}, u32[]{:S(2)}, u32[]{:S(2)}) collective-permute-start(f32[1,32,512]{2,1,0:T(8,128)} %get-tuple-element.11), channel_id=1, source_target_pairs={{16,0},{32,16},{48,32},{64,48},{80,64},{96,80},{112,96},{128,112},... | collective-permute-start | bytes 196616 | tf_op jit(solution)/shard_map/ppermute | solution.py:18
  177.6 147.8 %collective-permute-start.19 = (f32[1,32,512]{2,1,0:T(8,128)}, f32[1,32,512]{2,1,0:T(8,128)S(1)}, u32[]{:S(2)}, u32[]{:S(2)}) collective-permute-start(f32[1,32,512]{2,1,0:T(8,128)} %get-tuple-element.10), channel_id=1, source_target_pairs={{0,16},{16,32},{32,48},{48,64},{64,80},{80,96},{96,112},{112,128},... | collective-permute-start | bytes 196616 | tf_op jit(solution)/shard_map/ppermute | solution.py:15
  318.9 119.4 %collective-permute-start.22 = (f32[8,32,32]{2,1,0:T(8,128)}, f32[8,32,32]{2,1,0:T(8,128)S(1)}, u32[]{:S(2)}, u32[]{:S(2)}) collective-permute-start(f32[8,32,32]{2,1,0:T(8,128)} %get-tuple-element.12), channel_id=1, source_target_pairs={{2,0},{4,2},{6,4},{8,6},{10,8},{12,10},{14,12},{3,1},{5,3},{7,5},{... | collective-permute-start | bytes 98312 | tf_op jit(solution)/shard_map/ppermute | solution.py:18
  320.2 118.1 %collective-permute-start.23 = (f32[8,32,32]{2,1,0:T(8,128)}, f32[8,32,32]{2,1,0:T(8,128)}, u32[]{:S(2)}, u32[]{:S(2)}) collective-permute-start(f32[8,32,32]{2,1,0:T(8,128)} %get-tuple-element.13), channel_id=1, source_target_pairs={{0,2},{2,4},{4,6},{6,8},{8,10},{10,12},{12,14},{1,3},{3,5},{5,7},{... | collective-permute-start | bytes 98312 | tf_op jit(solution)/shard_map/ppermute | solution.py:15
  327.0 111.2 %collective-permute-start.20 = (f32[10,1,512]{2,1,0:T(1,128)}, f32[10,1,512]{2,1,0:T(1,128)S(1)}, u32[]{:S(2)}, u32[]{:S(2)}) collective-permute-start(f32[10,1,512]{2,1,0:T(1,128)} %get-tuple-element.2), channel_id=1, source_target_pairs={{1,0},{3,2},{5,4},{7,6},{9,8},{11,10},{13,12},{15,14},{17,16},{19,... | collective-permute-start | bytes 61448 | tf_op jit(solution)/shard_map/ppermute | solution.py:18
  328.3 110.0 %collective-permute-start.21 = (f32[10,1,512]{2,1,0:T(1,128)}, f32[10,1,512]{2,1,0:T(1,128)S(1)}, u32[]{:S(2)}, u32[]{:S(2)}) collective-permute-start(f32[10,1,512]{2,1,0:T(1,128)} %get-tuple-element.3), channel_id=1, source_target_pairs={{0,1},{2,3},{4,5},{6,7},{8,9},{10,11},{12,13},{14,15},{16,17},{18,... | collective-permute-start | bytes 61448 | tf_op jit(solution)/shard_map/ppermute | solution.py:15
  (1 other events, 0.8 us)
Sparse Core Ops, SparseCore 0:
  171.7 134.5 all-gather.3
  317.3 112.3 all-reduce.5
where the time goes:
time: 450 us; the launch traced here: 449 us
  waiting for transfers between devices  224 us (50%)
  starting transfers between devices  110 us (24%)
  blocking collectives  42.9 us (10%)
  local copies, waits for them, and re-layouts  30.8 us (7%)
  other arithmetic  16.1 us (4%)
  between operations  15.2 us (3%)
  matrix products  9.88 us (2%)
    all_gather x1, waiting for transfers between devices, body(): piece = lax.all_gather(block_traces[None], ('gx', 'gz'), axis=0, tiled=True)  118 us
    psum x1, waiting for transfers between devices, body(): total = lax.psum(partial_rows, 'gy')  98.3 us
    ppermute x12, starting transfers between devices, extended(): lax.ppermute(lax.slice_in_dim(block, block.shape[dim] - width, None, axis...  69.5 us
    all_gather x1, blocking collectives, body(): face_block = lax.all_gather(face_local, 'gy', axis=1, tiled=True)  42.9 us
    ppermute x12, starting transfers between devices, extended(): lax.ppermute(lax.slice_in_dim(block, 0, width, axis=dim), axis, backward)  40.3 us
    div x4, other arithmetic, sweep(): return (rhs + beside) / diag  11.1 us
  transfers between devices with their start and end apart: 26, of which 4 were waited for; matrix products, arithmetic and copies ran while one was open for 8% of the time, Pallas kernels for 0%

commit v1 on v0

--- a/solution.py
+++ b/solution.py
@@ -78,7 +78,7 @@
         preferred_element_type=jnp.float32,
     )
     partial_rows = nearpart + farpart
-    total = lax.psum(partial_rows, "gy")
+    total = jnp.sum(lax.all_gather(partial_rows, "gy"), axis=0)
     face_flux = total[:, perm].reshape(E, rows_x, cells_y * groups)
     mine = lax.dynamic_slice_in_dim(face_flux, mine_y * cells_y, cells_y, 2)
     flux_rows = mine.transpose(1, 2, 0).reshape(rows_x, cells_y * E)

time: 450 us -> 399 us (0.89)
  the two profiles are of different devices: /device:TPU:2 before, /device:TPU:6 now
where the time goes in v1:
time: 399 us; the launch traced here: 398 us
  waiting for transfers between devices  172 us (43%)
  starting transfers between devices  112 us (28%)
  blocking collectives  42.8 us (11%)
  local copies, waits for them, and re-layouts  29.2 us (7%)
  other arithmetic  17.3 us (4%)
  between operations  15.2 us (4%)
  matrix products  9.77 us (2%)
    all_gather x1, waiting for transfers between devices, body(): piece = lax.all_gather(block_traces[None], ('gx', 'gz'), axis=0, tiled=True)  129 us
    ppermute x12, starting transfers between devices, extended(): lax.ppermute(lax.slice_in_dim(block, block.shape[dim] - width, None, axis...  68.8 us
    all_gather x1, blocking collectives, body(): face_block = lax.all_gather(face_local, 'gy', axis=1, tiled=True)  42.8 us
    ppermute x12, starting transfers between devices, extended(): lax.ppermute(lax.slice_in_dim(block, 0, width, axis=dim), axis, backward)  42.7 us
    all_gather x1, waiting for transfers between devices, body(): total = jnp.sum(lax.all_gather(partial_rows, 'gy'), axis=0)  29.8 us
    ppermute x12, waiting for transfers between devices, extended(): lax.ppermute(lax.slice_in_dim(block, block.shape[dim] - width, None, axis...  12.7 us
    div x4, other arithmetic, sweep(): return (rhs + beside) / diag  11 us
  transfers between devices with their start and end apart: 26, of which 7 were waited for; matrix products, arithmetic and copies ran while one was open for 7% of the time, Pallas kernels for 0%

profile of v1, /device:TPU:6, one launch (start us, length us, event | category | flops | bytes accessed | tf_op | source)
XLA Modules:
  0.0 397.9 jit_solution(9854299509466809790)
XLA Ops:
  7.2 16.1 %collective-permute-start = (f32[1,32,512]{2,1,0:T(8,128)S(1)}, f32[1,32,512]{2,1,0:T(8,128)S(1)}, u32[]{:S(2)}, u32[]{:S(2)}) collective-permute-start(f32[1,32,512]{2,1,0:T(8,128)S(1)} %broadcast.45), channel_id=1, source_target_pairs={{16,0},{32,16},{48,32},{64,48},{80,64},{96,80},{112,96},{128,112},... | collective-permute-start | bytes 196616 | tf_op jit(solution)/shard_map/ppermute | solution.py:18
  23.4 1.9 collective-permute-start.1
  27.3 5.2 %collective-permute-start.5 = (f32[8,32,32]{2,1,0:T(8,128)}, f32[8,32,32]{2,1,0:T(8,128)}, u32[]{:S(2)}, u32[]{:S(2)}) collective-permute-start(f32[8,32,32]{2,1,0:T(8,128)} %broadcast.46), channel_id=1, source_target_pairs={{0,2},{2,4},{4,6},{6,8},{8,10},{10,12},{12,14},{1,3},{3,5},{5,7},{... | collective-permute-start | bytes 98312 | tf_op jit(solution)/shard_map/ppermute | solution.py:15
  32.5 7.2 %collective-permute-done.1 = f32[1,32,512]{2,1,0:T(8,128)S(1)} collective-permute-done((f32[1,32,512]{2,1,0:T(8,128)S(1)}, f32[1,32,512]{2,1,0:T(8,128)S(1)}, u32[]{:S(2)}, u32[]{:S(2)}) %collective-permute-start.1) | collective-permute-done | bytes 65568 | tf_op jit(solution)/shard_map/ppermute | solution.py:15
  41.0 3.0 collective-permute-start.3
  45.0 2.0 broadcast_in_dim.18
  47.0 2.3 reshape.71
  51.0 6.4 %collective-permute-start.6 = (f32[1,32,512]{2,1,0:T(8,128)S(1)}, f32[1,32,512]{2,1,0:T(8,128)S(1)}, u32[]{:S(2)}, u32[]{:S(2)}) collective-permute-start(f32[1,32,512]{2,1,0:T(8,128)S(1)} %get-tuple-element.19), channel_id=1, source_target_pairs={{16,0},{32,16},{48,32},{64,48},{80,64},{96,80},{112,96},{128,112},... | collective-permute-start | bytes 196616 | tf_op jit(solution)/shard_map/ppermute | solution.py:18
  57.4 8.2 %collective-permute-start.7 = (f32[1,32,512]{2,1,0:T(8,128)S(1)}, f32[1,32,512]{2,1,0:T(8,128)S(1)}, u32[]{:S(2)}, u32[]{:S(2)}) collective-permute-start(f32[1,32,512]{2,1,0:T(8,128)S(1)} %get-tuple-element.18), channel_id=1, source_target_pairs={{0,16},{16,32},{32,48},{48,64},{64,80},{80,96},{96,112},{112,128},... | collective-permute-start | bytes 196616 | tf_op jit(solution)/shard_map/ppermute | solution.py:15
  67.6 6.0 %collective-permute-start.11 = (f32[8,32,32]{2,1,0:T(8,128)}, f32[8,32,32]{2,1,0:T(8,128)S(1)}, u32[]{:S(2)}, u32[]{:S(2)}) collective-permute-start(f32[8,32,32]{2,1,0:T(8,128)} %get-tuple-element.21), channel_id=1, source_target_pairs={{0,2},{2,4},{4,6},{6,8},{8,10},{10,12},{12,14},{1,3},{3,5},{5,7},{... | collective-permute-start | bytes 98312 | tf_op jit(solution)/shard_map/ppermute | solution.py:15
  77.1 4.2 %collective-permute-start.9 = (f32[10,1,512]{2,1,0:T(1,128)}, f32[10,1,512]{2,1,0:T(1,128)}, u32[]{:S(2)}, u32[]{:S(2)}) collective-permute-start(f32[10,1,512]{2,1,0:T(1,128)} %get-tuple-element.7), channel_id=1, source_target_pairs={{0,1},{2,3},{4,5},{6,7},{8,9},{10,11},{12,13},{14,15},{16,17},{18,... | collective-permute-start | bytes 61448 | tf_op jit(solution)/shard_map/ppermute | solution.py:15
  82.0 4.3 %scatter_custom_fusion = s32[1024]{0:T(1024)S(1)} fusion(s32[1024]{0:T(1024)S(1)} %bitcast.40, s32[1024]{0:T(1024)S(1)} %iota.13, s32[]{:T(128)} %constant.10.clone.1), kind=kCustom, calls=%fused_computation.106 | custom fusion | bytes 4100 | tf_op jit(solution)/shard_map/scatter | solution.py:53
  86.3 2.9 fusion.31
  89.2 8.1 %collective-permute-start.12 = (f32[1,32,512]{2,1,0:T(8,128)S(1)}, f32[1,32,512]{2,1,0:T(8,128)S(1)}, u32[]{:S(2)}, u32[]{:S(2)}) collective-permute-start(f32[1,32,512]{2,1,0:T(8,128)S(1)} %get-tuple-element.15), channel_id=1, source_target_pairs={{16,0},{32,16},{48,32},{64,48},{80,64},{96,80},{112,96},{128,112},... | collective-permute-start | bytes 196616 | tf_op jit(solution)/shard_map/ppermute | solution.py:18
  97.3 6.5 %collective-permute-start.13 = (f32[1,32,512]{2,1,0:T(8,128)S(1)}, f32[1,32,512]{2,1,0:T(8,128)S(1)}, u32[]{:S(2)}, u32[]{:S(2)}) collective-permute-start(f32[1,32,512]{2,1,0:T(8,128)S(1)} %get-tuple-element.14), channel_id=1, source_target_pairs={{0,16},{16,32},{32,48},{48,64},{64,80},{80,96},{96,112},{112,128},... | collective-permute-start | bytes 196616 | tf_op jit(solution)/shard_map/ppermute | solution.py:15
  105.9 7.5 %collective-permute-start.17 = (f32[8,32,32]{2,1,0:T(8,128)}, f32[8,32,32]{2,1,0:T(8,128)S(1)}, u32[]{:S(2)}, u32[]{:S(2)}) collective-permute-start(f32[8,32,32]{2,1,0:T(8,128)} %get-tuple-element.17), channel_id=1, source_target_pairs={{0,2},{2,4},{4,6},{6,8},{8,10},{10,12},{12,14},{1,3},{3,5},{5,7},{... | collective-permute-start | bytes 98312 | tf_op jit(solution)/shard_map/ppermute | solution.py:15
  113.4 2.3 collective-permute-done.13
  117.6 4.2 %collective-permute-start.15 = (f32[10,1,512]{2,1,0:T(1,128)}, f32[10,1,512]{2,1,0:T(1,128)}, u32[]{:S(2)}, u32[]{:S(2)}) collective-permute-start(f32[10,1,512]{2,1,0:T(1,128)} %get-tuple-element.5), channel_id=1, source_target_pairs={{0,1},{2,3},{4,5},{6,7},{8,9},{10,11},{12,13},{14,15},{16,17},{18,... | collective-permute-start | bytes 61448 | tf_op jit(solution)/shard_map/ppermute | solution.py:15
  122.4 2.8 fusion.24
  126.1 42.8 %all-gather = bf16[8,1,4096]{2,1,0:T(2,128)(2,1)S(1)} all-gather(bf16[8,1,512]{2,1,0:T(2,128)(2,1)S(1)} %fusion.43), channel_id=2, replica_groups=mesh['gx'=32,'gy'=8,'gz'=2] {'gy'}, dimensions={2}, use_global_device_ids=true | all-gather | bytes 73728 | tf_op jit(solution)/shard_map/all_gather | solution.py:51
  169.4 4.3 %gather_fusion = bf16[1024,32]{1,0:T(8,128)(2,1)} fusion(bf16[1024,32]{1,0:T(8,128)(2,1)S(1)} %reshape.72, s32[1024]{0:T(1024)S(1)} %fusion.44), kind=kCustom, calls=%fused_computation | custom fusion | bytes 135168 | tf_op jit(solution)/shard_map/gather | solution.py:54
  176.4 129.2 %all-gather.6.cloned.1.call-done = bf16[2048,1024]{1,0:T(8,128)(2,1)} async-done(((bf16[32,1024]{1,0:T(8,128)(2,1)}), bf16[2048,1024]{1,0:T(8,128)(2,1)}) %all-gather.6.cloned.1.call-update) | async-done | bytes 4194320 | tf_op jit(solution)/shard_map/all_gather | solution.py:56
  305.6 6.7 %fusion.4 = bf16[8,32,1024]{2,0,1:T(8,128)(2,1)S(1)} fusion(bf16[64,32,1024]{2,1,0:T(8,128)(2,1)} %bitcast.36, s32[8]{0:T(128)S(1)} %pad_add_fusion), kind=kOutput, calls=%fused_computation.7 | convolution fusion | flops 33817088 | bytes 4718624 | tf_op jit(solution)/shard_map/cn,net->cet/dot_general | solution.py:59
  314.0 2.4 fusion.7
  317.3 1.9 collective-permute-start.18
  319.3 12.6 %collective-permute-start.19 = (f32[1,32,512]{2,1,0:T(8,128)S(1)}, f32[1,32,512]{2,1,0:T(8,128)S(1)}, u32[]{:S(2)}, u32[]{:S(2)}) collective-permute-start(f32[1,32,512]{2,1,0:T(8,128)S(1)} %get-tuple-element.10), channel_id=1, source_target_pairs={{0,16},{16,32},{32,48},{48,64},{64,80},{80,96},{96,112},{112,128},... | collective-permute-start | bytes 196616 | tf_op jit(solution)/shard_map/ppermute | solution.py:15
  331.9 1.7 fusion.51
  334.9 5.2 %collective-permute-start.23 = (f32[8,32,32]{2,1,0:T(8,128)}, f32[8,32,32]{2,1,0:T(8,128)}, u32[]{:S(2)}, u32[]{:S(2)}) collective-permute-start(f32[8,32,32]{2,1,0:T(8,128)} %get-tuple-element.13), channel_id=1, source_target_pairs={{0,2},{2,4},{4,6},{6,8},{8,10},{10,12},{12,14},{1,3},{3,5},{5,7},{... | collective-permute-start | bytes 98312 | tf_op jit(solution)/shard_map/ppermute | solution.py:15
  344.3 4.2 %collective-permute-start.21 = (f32[10,1,512]{2,1,0:T(1,128)}, f32[10,1,512]{2,1,0:T(1,128)}, u32[]{:S(2)}, u32[]{:S(2)}) collective-permute-start(f32[10,1,512]{2,1,0:T(1,128)} %get-tuple-element.3), channel_id=1, source_target_pairs={{0,1},{2,3},{4,5},{6,7},{8,9},{10,11},{12,13},{14,15},{16,17},{18,... | collective-permute-start | bytes 61448 | tf_op jit(solution)/shard_map/ppermute | solution.py:15
  348.6 29.8 %all-gather.8.cloned.1.call-done = f32[256,1024]{1,0:T(8,128)} async-done(((f32[32,1024]{1,0:T(8,128)}), f32[256,1024]{1,0:T(8,128)}) %all-gather.8.cloned.1.call-update) | async-done | bytes 1048592 | tf_op jit(solution)/shard_map/all_gather | solution.py:81
  380.7 5.1 %gather_fusion.1 = f32[1024,32]{1,0:T(8,128)} fusion(f32[32,1024]{0,1:T(8,128)} %copy.18, s32[1024]{0:T(1024)S(1)} %broadcast_clamp_fusion), kind=kCustom, calls=%fused_computation.1 | custom fusion | bytes 266240 | tf_op jit(solution)/shard_map/gather | solution.py:82
  387.4 3.7 fusion.17
  (83 shorter events, 32.1 us)
Async XLA Ops:
  7.2 306.1 %copy-start = (bf16[1,1,1,1024,1024]{4,3,2,1,0:T(8,128)(2,1)S(1)}, bf16[1,1,1,1024,1024]{4,3,2,1,0:T(8,128)(2,1)}, u32[]{:S(2)}) copy-start(bf16[1,1,1,1024,1024]{4,3,2,1,0:T(8,128)(2,1)} %param.13) | copy-start | bytes 6291460
  7.2 42.2 %copy-start.1 = (f32[8,32,512]{2,1,0:T(8,128)S(1)}, f32[8,32,512]{2,1,0:T(8,128)}, u32[]{:S(2)}) copy-start(f32[8,32,512]{2,1,0:T(8,128)} %param.8) | copy-start | bytes 1572868
  7.2 298.4 %all-gather.6.cloned.1.call-start = ((), (), s32[]{:S(2)}) async-start(), calls=%async_computation | async-start | bytes 4259840 | tf_op jit(solution)/shard_map/all_gather | solution.py:56
  7.2 25.2 %collective-permute-start = (f32[1,32,512]{2,1,0:T(8,128)S(1)}, f32[1,32,512]{2,1,0:T(8,128)S(1)}, u32[]{:S(2)}, u32[]{:S(2)}) collective-permute-start(f32[1,32,512]{2,1,0:T(8,128)S(1)} %broadcast.45), channel_id=1, source_target_pairs={{16,0},{32,16},{48,32},{64,48},{80,64},{96,80},{112,96},{128,112},... | collective-permute-start | bytes 196616 | tf_op jit(solution)/shard_map/ppermute | solution.py:18
  23.4 16.3 %collective-permute-start.1 = (f32[1,32,512]{2,1,0:T(8,128)S(1)}, f32[1,32,512]{2,1,0:T(8,128)S(1)}, u32[]{:S(2)}, u32[]{:S(2)}) collective-permute-start(f32[1,32,512]{2,1,0:T(8,128)S(1)} %broadcast.45), channel_id=1, source_target_pairs={{0,16},{16,32},{32,48},{48,64},{64,80},{80,96},{96,112},{112,128},... | collective-permute-start | bytes 196616 | tf_op jit(solution)/shard_map/ppermute | solution.py:15
  26.0 23.3 %collective-permute-start.4 = (f32[8,32,32]{2,1,0:T(8,128)}, f32[8,32,32]{2,1,0:T(8,128)}, u32[]{:S(2)}, u32[]{:S(2)}) collective-permute-start(f32[8,32,32]{2,1,0:T(8,128)} %broadcast.46), channel_id=1, source_target_pairs={{2,0},{4,2},{6,4},{8,6},{10,8},{12,10},{14,12},{3,1},{5,3},{7,5},{... | collective-permute-start | bytes 98312 | tf_op jit(solution)/shard_map/ppermute | solution.py:18
  27.3 22.1 %collective-permute-start.5 = (f32[8,32,32]{2,1,0:T(8,128)}, f32[8,32,32]{2,1,0:T(8,128)}, u32[]{:S(2)}, u32[]{:S(2)}) collective-permute-start(f32[8,32,32]{2,1,0:T(8,128)} %broadcast.46), channel_id=1, source_target_pairs={{0,2},{2,4},{4,6},{6,8},{8,10},{10,12},{12,14},{1,3},{3,5},{5,7},{... | collective-permute-start | bytes 98312 | tf_op jit(solution)/shard_map/ppermute | solution.py:15
  39.7 9.6 %collective-permute-start.2 = (f32[10,1,512]{2,1,0:T(1,128)S(1)}, f32[10,1,512]{2,1,0:T(1,128)S(1)}, u32[]{:S(2)}, u32[]{:S(2)}) collective-permute-start(f32[10,1,512]{2,1,0:T(1,128)S(1)} %get-tuple-element.8), channel_id=1, source_target_pairs={{1,0},{3,2},{5,4},{7,6},{9,8},{11,10},{13,12},{15,14},{17,16},{19,... | collective-permute-start | bytes 61448 | tf_op jit(solution)/shard_map/ppermute | solution.py:18
  41.0 8.3 %collective-permute-start.3 = (f32[10,1,512]{2,1,0:T(1,128)S(1)}, f32[10,1,512]{2,1,0:T(1,128)S(1)}, u32[]{:S(2)}, u32[]{:S(2)}) collective-permute-start(f32[10,1,512]{2,1,0:T(1,128)S(1)} %get-tuple-element.9), channel_id=1, source_target_pairs={{0,1},{2,3},{4,5},{6,7},{8,9},{10,11},{12,13},{14,15},{16,17},{18,... | collective-permute-start | bytes 61448 | tf_op jit(solution)/shard_map/ppermute | solution.py:15
  51.0 24.1 %copy-start.4 = (f32[8,32,512]{2,1,0:T(8,128)}, f32[8,32,512]{2,1,0:T(8,128)S(1)}, u32[]{:S(2)}) copy-start(f32[8,32,512]{2,1,0:T(8,128)S(1)} %fusion.14) | copy-start | bytes 1572868
  51.0 22.6 %collective-permute-start.6 = (f32[1,32,512]{2,1,0:T(8,128)S(1)}, f32[1,32,512]{2,1,0:T(8,128)S(1)}, u32[]{:S(2)}, u32[]{:S(2)}) collective-permute-start(f32[1,32,512]{2,1,0:T(8,128)S(1)} %get-tuple-element.19), channel_id=1, source_target_pairs={{16,0},{32,16},{48,32},{64,48},{80,64},{96,80},{112,96},{128,112},... | collective-permute-start | bytes 196616 | tf_op jit(solution)/shard_map/ppermute | solution.py:18
  57.4 17.7 %collective-permute-start.7 = (f32[1,32,512]{2,1,0:T(8,128)S(1)}, f32[1,32,512]{2,1,0:T(8,128)S(1)}, u32[]{:S(2)}, u32[]{:S(2)}) collective-permute-start(f32[1,32,512]{2,1,0:T(8,128)S(1)} %get-tuple-element.18), channel_id=1, source_target_pairs={{0,16},{16,32},{32,48},{48,64},{64,80},{80,96},{96,112},{112,128},... | collective-permute-start | bytes 196616 | tf_op jit(solution)/shard_map/ppermute | solution.py:15
  66.4 19.9 %collective-permute-start.10 = (f32[8,32,32]{2,1,0:T(8,128)}, f32[8,32,32]{2,1,0:T(8,128)S(1)}, u32[]{:S(2)}, u32[]{:S(2)}) collective-permute-start(f32[8,32,32]{2,1,0:T(8,128)} %get-tuple-element.20), channel_id=1, source_target_pairs={{2,0},{4,2},{6,4},{8,6},{10,8},{12,10},{14,12},{3,1},{5,3},{7,5},{... | collective-permute-start | bytes 98312 | tf_op jit(solution)/shard_map/ppermute | solution.py:18
  67.6 18.7 %collective-permute-start.11 = (f32[8,32,32]{2,1,0:T(8,128)}, f32[8,32,32]{2,1,0:T(8,128)S(1)}, u32[]{:S(2)}, u32[]{:S(2)}) collective-permute-start(f32[8,32,32]{2,1,0:T(8,128)} %get-tuple-element.21), channel_id=1, source_target_pairs={{0,2},{2,4},{4,6},{6,8},{8,10},{10,12},{12,14},{1,3},{3,5},{5,7},{... | collective-permute-start | bytes 98312 | tf_op jit(solution)/shard_map/ppermute | solution.py:15
  75.8 10.5 %collective-permute-start.8 = (f32[10,1,512]{2,1,0:T(1,128)}, f32[10,1,512]{2,1,0:T(1,128)}, u32[]{:S(2)}, u32[]{:S(2)}) collective-permute-start(f32[10,1,512]{2,1,0:T(1,128)} %get-tuple-element.6), channel_id=1, source_target_pairs={{1,0},{3,2},{5,4},{7,6},{9,8},{11,10},{13,12},{15,14},{17,16},{19,... | collective-permute-start | bytes 61448 | tf_op jit(solution)/shard_map/ppermute | solution.py:18
  77.1 9.3 %collective-permute-start.9 = (f32[10,1,512]{2,1,0:T(1,128)}, f32[10,1,512]{2,1,0:T(1,128)}, u32[]{:S(2)}, u32[]{:S(2)}) collective-permute-start(f32[10,1,512]{2,1,0:T(1,128)} %get-tuple-element.7), channel_id=1, source_target_pairs={{0,1},{2,3},{4,5},{6,7},{8,9},{10,11},{12,13},{14,15},{16,17},{18,... | collective-permute-start | bytes 61448 | tf_op jit(solution)/shard_map/ppermute | solution.py:15
  89.2 26.5 %copy-start.3 = (f32[8,32,512]{2,1,0:T(8,128)}, f32[8,32,512]{2,1,0:T(8,128)S(1)}, u32[]{:S(2)}) copy-start(f32[8,32,512]{2,1,0:T(8,128)S(1)} %fusion.31) | copy-start | bytes 1572868
  89.2 87.1 %copy-start.7 = (s32[1,1,1,7]{3,2,1,0:T(1,128)S(1)}, s32[1,1,1,7]{3,2,1,0:T(1,128)}, u32[]{:S(2)}) copy-start(s32[1,1,1,7]{3,2,1,0:T(1,128)} %param.12) | copy-start | bytes 88
  89.2 24.1 %collective-permute-start.12 = (f32[1,32,512]{2,1,0:T(8,128)S(1)}, f32[1,32,512]{2,1,0:T(8,128)S(1)}, u32[]{:S(2)}, u32[]{:S(2)}) collective-permute-start(f32[1,32,512]{2,1,0:T(8,128)S(1)} %get-tuple-element.15), channel_id=1, source_target_pairs={{16,0},{32,16},{48,32},{64,48},{80,64},{96,80},{112,96},{128,112},... | collective-permute-start | bytes 196616 | tf_op jit(solution)/shard_map/ppermute | solution.py:18
  97.3 18.3 %collective-permute-start.13 = (f32[1,32,512]{2,1,0:T(8,128)S(1)}, f32[1,32,512]{2,1,0:T(8,128)S(1)}, u32[]{:S(2)}, u32[]{:S(2)}) collective-permute-start(f32[1,32,512]{2,1,0:T(8,128)S(1)} %get-tuple-element.14), channel_id=1, source_target_pairs={{0,16},{16,32},{32,48},{48,64},{64,80},{80,96},{96,112},{112,128},... | collective-permute-start | bytes 196616 | tf_op jit(solution)/shard_map/ppermute | solution.py:15
  104.6 17.3 %collective-permute-start.16 = (f32[8,32,32]{2,1,0:T(8,128)}, f32[8,32,32]{2,1,0:T(8,128)S(1)}, u32[]{:S(2)}, u32[]{:S(2)}) collective-permute-start(f32[8,32,32]{2,1,0:T(8,128)} %get-tuple-element.16), channel_id=1, source_target_pairs={{2,0},{4,2},{6,4},{8,6},{10,8},{12,10},{14,12},{3,1},{5,3},{7,5},{... | collective-permute-start | bytes 98312 | tf_op jit(solution)/shard_map/ppermute | solution.py:18
  105.9 16.0 %collective-permute-start.17 = (f32[8,32,32]{2,1,0:T(8,128)}, f32[8,32,32]{2,1,0:T(8,128)S(1)}, u32[]{:S(2)}, u32[]{:S(2)}) collective-permute-start(f32[8,32,32]{2,1,0:T(8,128)} %get-tuple-element.17), channel_id=1, source_target_pairs={{0,2},{2,4},{4,6},{6,8},{8,10},{10,12},{12,14},{1,3},{3,5},{5,7},{... | collective-permute-start | bytes 98312 | tf_op jit(solution)/shard_map/ppermute | solution.py:15
  116.3 5.5 %collective-permute-start.14 = (f32[10,1,512]{2,1,0:T(1,128)}, f32[10,1,512]{2,1,0:T(1,128)}, u32[]{:S(2)}, u32[]{:S(2)}) collective-permute-start(f32[10,1,512]{2,1,0:T(1,128)} %get-tuple-element.4), channel_id=1, source_target_pairs={{1,0},{3,2},{5,4},{7,6},{9,8},{11,10},{13,12},{15,14},{17,16},{19,... | collective-permute-start | bytes 61448 | tf_op jit(solution)/shard_map/ppermute | solution.py:18
  117.6 4.8 %collective-permute-start.15 = (f32[10,1,512]{2,1,0:T(1,128)}, f32[10,1,512]{2,1,0:T(1,128)}, u32[]{:S(2)}, u32[]{:S(2)}) collective-permute-start(f32[10,1,512]{2,1,0:T(1,128)} %get-tuple-element.5), channel_id=1, source_target_pairs={{0,1},{2,3},{4,5},{6,7},{8,9},{10,11},{12,13},{14,15},{16,17},{18,... | collective-permute-start | bytes 61448 | tf_op jit(solution)/shard_map/ppermute | solution.py:15
  175.4 138.6 %copy-start.6 = (bf16[1,1,1,7,16,1024]{5,4,3,2,1,0:T(8,128)(2,1)S(1)}, bf16[1,1,1,7,16,1024]{5,4,3,2,1,0:T(8,128)(2,1)}, u32[]{:S(2)}) copy-start(bf16[1,1,1,7,16,1024]{5,4,3,2,1,0:T(8,128)(2,1)} %param.14) | copy-start | bytes 688132
  175.4 202.9 %all-gather.8.cloned.1.call-start = ((), (), s32[]{:S(2)}) async-start(), calls=%async_computation.1 | async-start | bytes 1179648 | tf_op jit(solution)/shard_map/all_gather | solution.py:81
  317.3 22.8 %collective-permute-start.18 = (f32[1,32,512]{2,1,0:T(8,128)S(1)}, f32[1,32,512]{2,1,0:T(8,128)S(1)}, u32[]{:S(2)}, u32[]{:S(2)}) collective-permute-start(f32[1,32,512]{2,1,0:T(8,128)S(1)} %get-tuple-element.11), channel_id=1, source_target_pairs={{16,0},{32,16},{48,32},{64,48},{80,64},{96,80},{112,96},{128,112},... | collective-permute-start | bytes 196616 | tf_op jit(solution)/shard_map/ppermute | solution.py:18
  319.3 22.2 %collective-permute-start.19 = (f32[1,32,512]{2,1,0:T(8,128)S(1)}, f32[1,32,512]{2,1,0:T(8,128)S(1)}, u32[]{:S(2)}, u32[]{:S(2)}) collective-permute-start(f32[1,32,512]{2,1,0:T(8,128)S(1)} %get-tuple-element.10), channel_id=1, source_target_pairs={{0,16},{16,32},{32,48},{48,64},{64,80},{80,96},{96,112},{112,128},... | collective-permute-start | bytes 196616 | tf_op jit(solution)/shard_map/ppermute | solution.py:15
  333.6 53.7 %collective-permute-start.22 = (f32[8,32,32]{2,1,0:T(8,128)}, f32[8,32,32]{2,1,0:T(8,128)S(1)}, u32[]{:S(2)}, u32[]{:S(2)}) collective-permute-start(f32[8,32,32]{2,1,0:T(8,128)} %get-tuple-element.12), channel_id=1, source_target_pairs={{2,0},{4,2},{6,4},{8,6},{10,8},{12,10},{14,12},{3,1},{5,3},{7,5},{... | collective-permute-start | bytes 98312 | tf_op jit(solution)/shard_map/ppermute | solution.py:18
  334.9 52.4 %collective-permute-start.23 = (f32[8,32,32]{2,1,0:T(8,128)}, f32[8,32,32]{2,1,0:T(8,128)}, u32[]{:S(2)}, u32[]{:S(2)}) collective-permute-start(f32[8,32,32]{2,1,0:T(8,128)} %get-tuple-element.13), channel_id=1, source_target_pairs={{0,2},{2,4},{4,6},{6,8},{8,10},{10,12},{12,14},{1,3},{3,5},{5,7},{... | collective-permute-start | bytes 98312 | tf_op jit(solution)/shard_map/ppermute | solution.py:15
  343.1 44.3 %collective-permute-start.20 = (f32[10,1,512]{2,1,0:T(1,128)}, f32[10,1,512]{2,1,0:T(1,128)}, u32[]{:S(2)}, u32[]{:S(2)}) collective-permute-start(f32[10,1,512]{2,1,0:T(1,128)} %get-tuple-element.2), channel_id=1, source_target_pairs={{1,0},{3,2},{5,4},{7,6},{9,8},{11,10},{13,12},{15,14},{17,16},{19,... | collective-permute-start | bytes 61448 | tf_op jit(solution)/shard_map/ppermute | solution.py:18
  344.3 43.0 %collective-permute-start.21 = (f32[10,1,512]{2,1,0:T(1,128)}, f32[10,1,512]{2,1,0:T(1,128)}, u32[]{:S(2)}, u32[]{:S(2)}) collective-permute-start(f32[10,1,512]{2,1,0:T(1,128)} %get-tuple-element.3), channel_id=1, source_target_pairs={{0,1},{2,3},{4,5},{6,7},{8,9},{10,11},{12,13},{14,15},{16,17},{18,... | collective-permute-start | bytes 61448 | tf_op jit(solution)/shard_map/ppermute | solution.py:15
  (2 other events, 6.1 us)
Sparse Core Ops, SparseCore 0:
  175.6 129.9 all-gather.5
  316.5 61.8 all-gather.7
